TPU v7x, 32 devices: a whole 2x2x4 slice. The times are simulated.
32 devices in a mesh: ctx: 8 (over y, x, core), wshard: 4 (over z).
Axes of the slice: x: 2, y: 2, z: 4, core: 2. Of those that a mesh axis runs over, the one named last changes fastest.
Arguments:
- byte_feats: bfloat16 [8, 2048, 768], P('wshard', 'ctx'), may hold values from -6 to 6
- lengths: int32 [8], P('wshard'), may hold values from 512 to 2048, as said below
- latent_array: bfloat16 [256, 1280], P('wshard'), may hold values from -6 to 6
- lat_gain: bfloat16 [1280], P('wshard'), may hold values from 0.5 to 1.5
- lat_bias: bfloat16 [1280], P('wshard'), may hold values from -4 to 4
- in_gain: bfloat16 [768], P('wshard'), may hold values from 0.5 to 1.5
- in_bias: bfloat16 [768], P('wshard'), may hold values from -4 to 4
- w_query: bfloat16 [1280, 256], P('wshard'), may hold values from -0.25 to 0.25
- w_key: bfloat16 [768, 256], P('wshard'), may hold values from -0.3125 to 0.3125
- w_value: bfloat16 [768, 1280], P('wshard'), may hold values from -0.21875 to 0.21875
- w_output: bfloat16 [1280, 1280], P('wshard'), may hold values from -2 to 2
- mlp_gain: bfloat16 [1280], P('wshard'), may hold values from 0.5 to 1.5
- mlp_bias: bfloat16 [1280], P('wshard'), may hold values from -4 to 4
- w_up: bfloat16 [1280, 1280], P('wshard'), may hold values from -0.15625 to 0.15625
- w_down: bfloat16 [1280, 1280], P('wshard'), may hold values from -0.15625 to 0.15625
- cotangent: bfloat16 [8, 256, 1280], P('wshard'), may hold values from -6 to 6
Outputs:
- latents_out: bfloat16 [8, 256, 1280], P('wshard')
- byte_grad: bfloat16 [8, 2048, 768], P('wshard', 'ctx')
- grad_latent: float32 [256, 1280], P('wshard')
- grad_lat_gain: float32 [1280], P('wshard')
- grad_lat_bias: float32 [1280], P('wshard')
- grad_in_gain: float32 [768], P('wshard')
- grad_in_bias: float32 [768], P('wshard')
- grad_query: float32 [1280, 256], P('wshard')
- grad_key: float32 [768, 256], P('wshard')
- grad_value: float32 [768, 1280], P('wshard')
- grad_output: float32 [1280, 1280], P('wshard')
- grad_mlp_gain: float32 [1280], P('wshard')
- grad_mlp_bias: float32 [1280], P('wshard')
- grad_up: float32 [1280, 1280], P('wshard')
- grad_down: float32 [1280, 1280], P('wshard')
Inputs may be any that keep to these rules, and one draw needn't show every extreme that they name: The first lengths[s] slots of sequence s hold bytes, the rest are padding; some sequence fills all 2048 slots.
All inputs are finite; a program needn't handle non-finite values.
Results may differ from a plain program's by a relative error of at most 0.019.
Values may be sent and summed in bfloat16 or wider, within the bound.
A program may use at most 256 MiB of HBM per device.

v0:
```python
import math
import jax
import jax.numpy as jnp
from jax import lax
from jax.sharding import PartitionSpec as P

H = 8
LOW = jnp.bfloat16
FULL = jnp.float32


def layer_norm(values, gain, offset):
    center = jnp.mean(values, axis=-1, keepdims=True)
    centred = values - center
    variance = jnp.mean(centred * centred, axis=-1, keepdims=True)
    return centred * lax.rsqrt(variance + 1e-05) * gain + offset


def exact_gelu(values):
    return jax.nn.gelu(values, approximate=False)


def matmul(left, right):
    return jnp.dot(left, right, preferred_element_type=FULL)


def matmul_tn(left, right):
    return lax.dot_general(left, right, (((0,), (0,)), ((), ())), preferred_element_type=FULL)


def matmul_nt(left, right):
    return lax.dot_general(left, right, (((1,), (1,)), ((), ())), preferred_element_type=FULL)


def gather(shard):
    return lax.all_gather(shard, "wshard", axis=0, tiled=True)


def scatter(total):
    return lax.psum_scatter(total.astype(LOW), "wshard", scatter_dimension=0, tiled=True).astype(
        FULL
    )


def own_part(total, shard):
    size = shard.shape[0]
    return lax.dynamic_slice_in_dim(total, lax.axis_index("wshard") * size, size, 0)


def shards(
    byte_feats,
    lengths,
    latent_array,
    lat_gain,
    lat_bias,
    in_gain,
    in_bias,
    w_query,
    w_key,
    w_value,
    w_output,
    mlp_gain,
    mlp_bias,
    w_up,
    w_down,
    cotangent,
):
    seqs, slots, width = byte_feats.shape
    gain_in, bias_in = (gather(in_gain).astype(FULL), gather(in_bias).astype(FULL))
    key_w, value_w = (gather(w_key), gather(w_value))
    latent = gather(latent_array).astype(FULL)
    gain_lat, bias_lat = (gather(lat_gain).astype(FULL), gather(lat_bias).astype(FULL))
    query_w = gather(w_query)
    gain_mlp, bias_mlp = (gather(mlp_gain).astype(FULL), gather(mlp_bias).astype(FULL))
    output_w, up_w, down_w = (gather(w_output), gather(w_up), gather(w_down))
    features = byte_feats.reshape(seqs * slots, width).astype(FULL)
    normed_in, in_back = jax.vjp(layer_norm, features, gain_in, bias_in)
    input_low = normed_in.astype(LOW)
    keys = matmul(input_low, key_w).astype(LOW)
    values = matmul(input_low, value_w).astype(LOW)
    normed_lat, lat_back = jax.vjp(layer_norm, latent, gain_lat, bias_lat)
    lat_low = normed_lat.astype(LOW)
    rows = lat_low.shape[0]
    queries = matmul(lat_low, query_w).astype(LOW)
    score_scale = 1.0 / math.sqrt(queries.shape[1] // H)
    qheads = queries.reshape(rows, H, -1)
    kheads = keys.reshape(seqs, slots, H, -1)
    vheads = values.reshape(seqs, slots, H, -1)
    scores = jnp.einsum("lhd,mkhd->mhlk", qheads, kheads, preferred_element_type=FULL) * score_scale
    slot_ids = lax.axis_index("ctx") * slots + lax.iota(jnp.int32, slots)
    valid = (slot_ids[None, :] < lengths[:, None])[:, None, None, :]
    scores = jnp.where(valid, scores, -1e30)
    highest = lax.pmax(jnp.max(scores, axis=-1), "ctx")
    weights = jnp.where(valid, jnp.exp(scores - highest[..., None]), 0.0)
    total = lax.psum(jnp.sum(weights, axis=-1), "ctx")
    numer = jnp.einsum("mhlk,mkhe->mlhe", weights.astype(LOW), vheads, preferred_element_type=FULL)
    numer = lax.psum(numer.astype(LOW), "ctx").astype(FULL)
    attended = numer / jnp.transpose(total, (0, 2, 1))[..., None]
    attended = attended.reshape(seqs * rows, -1)
    att_low = attended.astype(LOW)
    hidden = jnp.tile(latent, (seqs, 1)) + matmul(att_low, output_w)
    normed_mid, mid_back = jax.vjp(layer_norm, hidden, gain_mlp, bias_mlp)
    mid_low = normed_mid.astype(LOW)
    upward = matmul(mid_low, up_w)
    activated, gelu_back = jax.vjp(exact_gelu, upward)
    act_low = activated.astype(LOW)
    result = hidden + matmul(act_low, down_w)
    dout_low = cotangent.reshape(seqs * rows, -1)
    grad_down = scatter(matmul_tn(act_low, dout_low))
    (grad_upward,) = gelu_back(matmul_nt(dout_low, down_w))
    up_low = grad_upward.astype(LOW)
    grad_up = scatter(matmul_tn(mid_low, up_low))
    dhid_norm, grad_gmlp, grad_bmlp = mid_back(matmul_nt(up_low, up_w))
    dhidden = dout_low.astype(FULL) + dhid_norm
    dhid_low = dhidden.astype(LOW)
    grad_output = scatter(matmul_tn(att_low, dhid_low))
    grad_hidden = scatter(jnp.sum(dhidden.reshape(seqs, rows, -1), axis=0))
    grad_att = matmul_nt(dhid_low, output_w).astype(LOW)
    grad_heads = grad_att.reshape(seqs, rows, H, -1)
    delta = jnp.sum(
        grad_heads.astype(FULL) * attended.reshape(seqs, rows, H, -1), axis=-1
    ).transpose(0, 2, 1)
    probs = weights / total[..., None]
    dprobs = jnp.einsum("mlhe,mkhe->mhlk", grad_heads, vheads, preferred_element_type=FULL)
    dscores = (probs * (dprobs - delta[..., None])).astype(LOW)
    dquery = (
        jnp.einsum("mhlk,mkhd->lhd", dscores, kheads, preferred_element_type=FULL) * score_scale
    )
    dkeys = jnp.einsum("mhlk,lhd->mkhd", dscores, qheads, preferred_element_type=FULL) * score_scale
    dvalues = jnp.einsum(
        "mhlk,mlhe->mkhe", probs.astype(LOW), grad_heads, preferred_element_type=FULL
    )
    dkeys = dkeys.astype(LOW).reshape(seqs * slots, -1)
    dvalues = dvalues.astype(LOW).reshape(seqs * slots, -1)
    dquery = lax.psum(dquery.reshape(rows, -1).astype(LOW), ("ctx", "wshard"))
    grad_query = matmul_tn(
        lax.dynamic_slice_in_dim(
            lat_low, lax.axis_index("wshard") * w_query.shape[0], w_query.shape[0], 1
        ),
        dquery,
    )
    dlat_norm, grad_glat, grad_blat = lat_back(matmul_nt(dquery, query_w))
    grad_latent = grad_hidden + own_part(dlat_norm, latent_array)
    dnorm_in = matmul_nt(dkeys, key_w) + matmul_nt(dvalues, value_w)
    dfeatures, grad_gin, grad_bin = in_back(dnorm_in)
    grad_key = lax.psum(scatter(matmul_tn(input_low, dkeys)).astype(LOW), "ctx").astype(FULL)
    grad_value = lax.psum(scatter(matmul_tn(input_low, dvalues)).astype(LOW), "ctx").astype(FULL)
    in_sums = lax.psum(jnp.concatenate([grad_gin, grad_bin]), ("ctx", "wshard"))
    grad_gin, grad_bin = jnp.split(in_sums, 2)
    mlp_sums = lax.psum(jnp.concatenate([grad_gmlp, grad_bmlp]), "wshard")
    grad_gmlp, grad_bmlp = jnp.split(mlp_sums, 2)
    return (
        result.astype(LOW).reshape(seqs, rows, -1),
        dfeatures.astype(LOW).reshape(seqs, slots, width),
        grad_latent,
        own_part(grad_glat, lat_gain),
        own_part(grad_blat, lat_bias),
        own_part(grad_gin, in_gain),
        own_part(grad_bin, in_bias),
        grad_query,
        grad_key,
        grad_value,
        grad_output,
        own_part(grad_gmlp, mlp_gain),
        own_part(grad_bmlp, mlp_bias),
        grad_up,
        grad_down,
    )


def solution(mesh):
    sharded, plain = (P("wshard", None), P("wshard"))
    return jax.shard_map(
        shards,
        mesh=mesh,
        in_specs=(
            P("wshard", "ctx", None),
            plain,
            sharded,
            plain,
            plain,
            plain,
            plain,
            sharded,
            sharded,
            sharded,
            sharded,
            plain,
            plain,
            sharded,
            sharded,
            P("wshard", None, None),
        ),
        out_specs=(
            P("wshard", None, None),
            P("wshard", "ctx", None),
            sharded,
            plain,
            plain,
            plain,
            plain,
            sharded,
            sharded,
            sharded,
            sharded,
            plain,
            plain,
            sharded,
            sharded,
        ),
        check_vma=False,
    )
```

profile of v0, /device:TPU:0, one launch (start us, length us, event | category | flops | bytes accessed | tf_op | source)
XLA Modules:
  0.0 920.5 jit_solution(9357087982869084946)
XLA Ops:
  8.1 22.5 %all_gather.39 = bf16[256,1280]{1,0:T(8,128)(2,1)S(1)} all-gather(bf16[64,1280]{1,0:T(8,128)(2,1)} %param.18), channel_id=1, replica_groups=mesh['ctx'=8,'wshard'=4] {'wshard'}, dimensions={0}, use_global_device_ids=true | all-gather | bytes 819200 | tf_op jit(solution)/shard_map/all_gather | solution.py:36
  30.5 1.2 dynamic-slice.4
  35.1 19.8 %all-reduce.7 = (bf16[1280]{0:T(1024)(128)(2,1)S(1)}, bf16[1280]{0:T(1024)(128)(2,1)S(1)}, bf16[768]{0:T(1024)(128)(2,1)S(1)}, bf16[768]{0:T(1024)(128)(2,1)S(1)...) all-reduce(bf16[1280]{0:T(1024)(128)(2,1)S(1)} %dynamic-update-slic, ...), channel_id=1, replica_groups=mesh['ctx'=8,'wshard'=4] {'wshard'}, use_global_device_ids=true, to_apply=%add.3 | all-reduce | flops 6656 | bytes 26624
  56.1 15.5 %all_gather.43 = bf16[768,256]{1,0:T(8,128)(2,1)S(1)} all-gather(bf16[192,256]{1,0:T(8,128)(2,1)S(1)} %copy-done.36), channel_id=1, replica_groups=mesh['ctx'=8,'wshard'=4] {'wshard'}, dimensions={0}, use_global_device_ids=true | all-gather | bytes 491520 | tf_op jit(solution)/shard_map/all_gather | solution.py:36
  73.1 15.1 %all_gather.46 = bf16[1280,256]{1,0:T(8,128)(2,1)S(1)} all-gather(bf16[320,256]{1,0:T(8,128)(2,1)S(1)} %copy-done.30), channel_id=1, replica_groups=mesh['ctx'=8,'wshard'=4] {'wshard'}, dimensions={0}, use_global_device_ids=true | all-gather | bytes 819200 | tf_op jit(solution)/shard_map/all_gather | solution.py:36
  90.5 3.0 bitcast_reduce_fusion
  93.5 22.3 %pmax.7 = f32[2,8,256]{2,0,1:T(2,128)S(1)} all-reduce(f32[2,8,256]{2,0,1:T(2,128)S(1)} %get-tuple-element.50), channel_id=1, replica_groups=mesh['ctx'=8,'wshard'=4] {'ctx'}, use_global_device_ids=true, to_apply=%region_5.6 | all-reduce | flops 4096 | bytes 32768 | tf_op jit(solution)/shard_map/pmax | solution.py:93
  115.8 3.4 fusion.37
  119.2 22.3 %psum.50 = f32[2,8,256]{2,0,1:T(2,128)S(1)} all-reduce(f32[2,8,256]{2,0,1:T(2,128)S(1)} %fusion.37), channel_id=1, replica_groups=mesh['ctx'=8,'wshard'=4] {'ctx'}, use_global_device_ids=true, to_apply=%region_8.9 | all-reduce | flops 4096 | bytes 32768 | tf_op jit(solution)/shard_map/psum | solution.py:95
  141.6 4.4 fusion.14
  146.0 3.8 convolution_convert_fusion.4
  149.8 1.6 copy.60
  151.4 1.2 reshape.259
  152.6 3.6 fusion.24
  158.4 1.2 add_convert_fusion.2
  159.7 53.1 %all-reduce.12.cloned.1.call-done = bf16[2,256,8,160]{1,3,2,0:T(8,128)(2,1)} async-done(((bf16[2,256,8,160]{1,3,2,0:T(8,128)(2,1)}), bf16[2,256,8,160]{1,3,2,0:T(8,128)(2,1)}) %all-reduce.12.cloned.1.call-update) | async-done | bytes 1310736 | tf_op jit(solution)/shard_map/psum | solution.py:97
  212.7 1.6 fusion.13
  214.3 1.4 copy.66
  216.0 63.3 %all-gather.7.cloned.1.call-done = bf16[1280,1280]{1,0:T(8,128)(2,1)} async-done(((bf16[320,1280]{1,0:T(8,128)(2,1)}), bf16[1280,1280]{1,0:T(8,128)(2,1)}) %all-gather.7.cloned.1.call-update) | async-done | bytes 3276816 | tf_op jit(solution)/shard_map/all_gather | solution.py:36
  279.5 1.8 copy-done.12
  281.2 2.1 fusion.58
  283.3 1.4 copy-done.1
  285.2 60.0 %all-gather.9.cloned.1.call-done = bf16[1280,1280]{1,0:T(8,128)(2,1)} async-done(((bf16[320,1280]{1,0:T(8,128)(2,1)}), bf16[1280,1280]{1,0:T(8,128)(2,1)}) %all-gather.9.cloned.1.call-update) | async-done | bytes 3276816 | tf_op jit(solution)/shard_map/all_gather | solution.py:36
  345.1 6.2 fusion.51
  351.4 59.6 %all-gather.11.cloned.1.call-done = bf16[1280,1280]{1,0:T(8,128)(2,1)} async-done(((bf16[320,1280]{1,0:T(8,128)(2,1)}), bf16[1280,1280]{1,0:T(8,128)(2,1)}) %all-gather.11.cloned.1.call-update) | async-done | bytes 3276816 | tf_op jit(solution)/shard_map/all_gather | solution.py:36
  410.9 11.0 %add_convert_fusion = (bf16[512,1280]{1,0:T(8,128)(2,1)S(1)}, f32[512,1280]{1,0:T(8,128)}) fusion(f32[512,1280]{1,0:T(8,128)} %fusion.51, bf16[512,1280]{1,0:T(8,128)(2,1)S(1)} %bitcast.132, bf16[1280,1280]{1,0:T(8,128)(2,1)} %all-gather.11.cloned.1.call-done), kind=kOutput, calls=%fused_computation.22 | convolution fusion | flops 1724907520 | bytes 11141120 | tf_op jit(solution)/shard_map/dot_general | solution.py:32
  421.9 2.8 multiply_reduce_fusion
  425.9 1.6 copy-done.4
  428.4 3.0 convolution_convert_fusion.5
  431.3 2.5 copy.67
  433.9 4.0 reshape.264
  437.9 1.9 multiply_reduce_fusion.1
  440.0 4.2 multiply_convert_fusion
  446.0 1.2 convolution_convert_fusion.6
  447.3 2.8 fusion.21
  450.1 1.4 copy.77
  452.8 2.6 convolution_convert_fusion.3
  455.4 2.0 fusion.34
  457.6 3.1 reduce_sum.204
  460.7 5.9 reduce-scatter.9.cloned.1.call-done
  466.6 42.1 %reduce-scatter.11.cloned.1.call-done = bf16[192,1280]{1,0:T(8,128)(2,1)} async-done(((bf16[768,1280]{1,0:T(8,128)(2,1)}), bf16[192,1280]{1,0:T(8,128)(2,1)}) %reduce-scatter.11.cloned.1.call-update) | async-done | bytes 491536 | tf_op jit(solution)/shard_map/reduce_scatter | solution.py:40
  508.7 5.3 convolution_convert_fusion.2
  515.4 5.7 convolution_convert_fusion.1
  521.3 3.0 multiply_convert_fusion.1
  525.3 3.7 convolution_convert_fusion
  529.1 1.3 copy-done.22
  530.4 2.8 fusion.59
  534.3 39.6 %psum.52 = f32[1536]{0:T(1024)S(1)} all-reduce(f32[1536]{0:T(1024)S(1)} %pad_maximum_fusion.1), channel_id=1, replica_groups=mesh['ctx'=8,'wshard'=4] {'ctx','wshard'}, use_global_device_ids=true, to_apply=%region_25.26 | all-reduce | flops 1536 | bytes 12288 | tf_op jit(solution)/shard_map/psum | solution.py:148
  575.1 17.7 %psum.55 = f32[2560]{0:T(1024)S(1)} all-reduce(f32[2560]{0:T(1024)S(1)} %pad_maximum_fusion), channel_id=1, replica_groups=mesh['ctx'=8,'wshard'=4] {'wshard'}, use_global_device_ids=true, to_apply=%region_33.34 | all-reduce | flops 2560 | bytes 20480 | tf_op jit(solution)/shard_map/psum | solution.py:150
  596.5 5.0 fusion.2
  601.5 35.1 %all-reduce.14.cloned.1.call-done = bf16[256,256]{0,1:T(8,128)(2,1)} async-done(((bf16[256,256]{0,1:T(8,128)(2,1)}), bf16[256,256]{0,1:T(8,128)(2,1)}) %all-reduce.14.cloned.1.call-update) | async-done | bytes 131088 | tf_op jit(solution)/shard_map/psum | solution.py:135
  636.6 1.7 multiply_reduce_fusion.7
  640.3 2.0 fusion.43
  642.3 18.4 %reduce-scatter.7.cloned.1.call-done = bf16[64,1280]{1,0:T(8,128)(2,1)} async-done(((bf16[256,1280]{1,0:T(8,128)(2,1)}), bf16[64,1280]{1,0:T(8,128)(2,1)}) %reduce-scatter.7.cloned.1.call-update) | async-done | bytes 163856 | tf_op jit(solution)/shard_map/reduce_scatter | solution.py:40
  660.7 1.7 fusion.39
  662.5 55.3 %all-reduce.16.cloned.1.call-done = (bf16[192,256]{1,0:T(8,128)(2,1)}, bf16[192,1280]{1,0:T(8,128)(2,1)}) async-done(((bf16[192,256]{1,0:T(8,128)(2,1)}, bf16[192,1280]{1,0:T(8,128)(2,1)}), (bf16[192,256]{1,0:T(8,128)(2,1)}, bf16[192,1280]{1,0:T(8,128)(2,1)})) %all-reduce.16.cloned.1.call-update) | async-done | bytes 589840 | tf_op jit(solution)/shard_map/psum | solution.py:146
  717.8 1.6 convert_element_type.210
  719.3 2.0 convert_element_type.212
  721.4 60.4 %reduce-scatter.13.cloned.1.call-done = bf16[320,1280]{1,0:T(8,128)(2,1)} async-done(((bf16[1280,1280]{1,0:T(8,128)(2,1)}), bf16[320,1280]{1,0:T(8,128)(2,1)}) %reduce-scatter.13.cloned.1.call-update) | async-done | bytes 819216 | tf_op jit(solution)/shard_map/reduce_scatter | solution.py:40
  781.7 2.4 convert_element_type.214
  784.2 62.3 %reduce-scatter.15.cloned.1.call-done = bf16[320,1280]{1,0:T(8,128)(2,1)} async-done(((bf16[1280,1280]{1,0:T(8,128)(2,1)}), bf16[320,1280]{1,0:T(8,128)(2,1)}) %reduce-scatter.15.cloned.1.call-update) | async-done | bytes 819216 | tf_op jit(solution)/shard_map/reduce_scatter | solution.py:40
  846.5 2.4 convert_element_type.216
  848.9 62.4 %reduce-scatter.17.cloned.1.call-done = bf16[320,1280]{1,0:T(8,128)(2,1)} async-done(((bf16[1280,1280]{1,0:T(8,128)(2,1)}), bf16[320,1280]{1,0:T(8,128)(2,1)}) %reduce-scatter.17.cloned.1.call-update) | async-done | bytes 819216 | tf_op jit(solution)/shard_map/reduce_scatter | solution.py:40
  911.3 2.4 convert_element_type.218
  (240 shorter events, 26.7 us)
Async XLA Ops:
  7.2 26.4 %copy-start.63 = (bf16[320]{0:T(512)(128)(2,1)S(1)}, bf16[320]{0:T(512)(128)(2,1)}, u32[]{:S(2)}) copy-start(bf16[320]{0:T(512)(128)(2,1)} %param.20) | copy-start | bytes 1924
  7.2 26.7 %copy-start.64 = (bf16[320]{0:T(512)(128)(2,1)S(1)}, bf16[320]{0:T(512)(128)(2,1)}, u32[]{:S(2)}) copy-start(bf16[320]{0:T(512)(128)(2,1)} %param.19) | copy-start | bytes 1924
  7.2 26.9 %copy-start.69 = (bf16[192]{0:T(256)(128)(2,1)S(1)}, bf16[192]{0:T(256)(128)(2,1)}, u32[]{:S(2)}) copy-start(bf16[192]{0:T(256)(128)(2,1)} %param.22) | copy-start | bytes 1156
  7.2 27.2 %copy-start.70 = (bf16[192]{0:T(256)(128)(2,1)S(1)}, bf16[192]{0:T(256)(128)(2,1)}, u32[]{:S(2)}) copy-start(bf16[192]{0:T(256)(128)(2,1)} %param.21) | copy-start | bytes 1156
  7.2 27.4 %copy-start.65 = (bf16[320]{0:T(512)(128)(2,1)S(1)}, bf16[320]{0:T(512)(128)(2,1)}, u32[]{:S(2)}) copy-start(bf16[320]{0:T(512)(128)(2,1)} %param.28) | copy-start | bytes 1924
  7.2 27.6 %copy-start.66 = (bf16[320]{0:T(512)(128)(2,1)S(1)}, bf16[320]{0:T(512)(128)(2,1)}, u32[]{:S(2)}) copy-start(bf16[320]{0:T(512)(128)(2,1)} %param.27) | copy-start | bytes 1924
  7.2 47.6 %copy-start = (bf16[2,256,768]{2,1,0:T(8,128)(2,1)S(1)}, bf16[2,256,768]{2,1,0:T(8,128)(2,1)}, u32[]{:S(2)}) copy-start(bf16[2,256,768]{2,1,0:T(8,128)(2,1)} %param.16) | copy-start | bytes 2359300
  7.3 48.8 %copy-start.36 = (bf16[192,256]{1,0:T(8,128)(2,1)S(1)}, bf16[192,256]{1,0:T(8,128)(2,1)}, u32[]{:S(2)}) copy-start(bf16[192,256]{1,0:T(8,128)(2,1)} %param.24) | copy-start | bytes 294916
  7.3 138.7 %all-gather.5.cloned.1.call-start = ((), (), s32[]{:S(2)}) async-start(), calls=%async_computation.6 | async-start | bytes 2457600 | tf_op jit(solution)/shard_map/all_gather | solution.py:36
  8.0 204.7 %all-reduce.12.cloned.1.call-start = ((), (), s32[]{:S(2)}) async-start(), calls=%async_computation.7 | async-start | bytes 2621440 | tf_op jit(solution)/shard_map/psum | solution.py:97
  33.3 55.0 %copy-start.51 = (f32[256]{0:T(256)}, f32[256]{0:T(256)S(1)}, u32[]{:S(2)}) copy-start(f32[256]{0:T(256)S(1)} %broadcast_multiply_fusion.2) | copy-start | bytes 3076
  33.6 39.1 %copy-start.55 = (f32[256]{0:T(256)}, f32[256]{0:T(256)S(1)}, u32[]{:S(2)}) copy-start(f32[256]{0:T(256)S(1)} %multiply_reduce_fusion.9) | copy-start | bytes 3076
  54.9 103.5 %copy-start.34 = (f32[768]{0:T(1024)}, f32[768]{0:T(1024)S(1)}, u32[]{:S(2)}) copy-start(f32[768]{0:T(1024)S(1)} %convert_element_type.170) | copy-start | bytes 9220
  55.1 18.0 %copy-start.67 = (s32[2]{0:T(128)S(1)}, s32[2]{0:T(128)}, u32[]{:S(2)}) copy-start(s32[2]{0:T(128)} %param.17) | copy-start | bytes 28
  55.1 18.0 %copy-start.30 = (bf16[320,256]{1,0:T(8,128)(2,1)S(1)}, bf16[320,256]{1,0:T(8,128)(2,1)}, u32[]{:S(2)}) copy-start(bf16[320,256]{1,0:T(8,128)(2,1)} %param.23) | copy-start | bytes 491524
  56.1 16.7 %copy-start.41 = (f32[512]{0:T(512)}, f32[512]{0:T(512)S(1)}, u32[]{:S(2)}) copy-start(f32[512]{0:T(512)S(1)} %rsqrt.33) | copy-start | bytes 6148
  56.1 16.7 %copy-start.43 = (f32[1,2,2,128]{3,1,2,0:T(2,128)}, f32[1,2,2,128]{3,1,2,0:T(2,128)S(1)}, u32[]{:S(2)}) copy-start(f32[1,2,2,128]{3,1,2,0:T(2,128)S(1)} %copy.93) | copy-start | bytes 6148
  72.7 20.7 %copy-start.53 = (f32[256]{0:T(256)}, f32[256]{0:T(256)S(1)}, u32[]{:S(2)}) copy-start(f32[256]{0:T(256)S(1)} %fusion.48) | copy-start | bytes 3076
  72.8 20.7 %copy-start.37 = (f32[1280]{0:T(1024)}, f32[1280]{0:T(1024)S(1)}, u32[]{:S(2)}) copy-start(f32[1280]{0:T(1024)S(1)} %convert_element_type.175) | copy-start | bytes 15364
  73.0 20.5 %copy-start.18 = (bf16[2,256,8,32]{1,0,3,2:T(2,128)(2,1)}, bf16[2,256,8,32]{1,0,3,2:T(2,128)(2,1)S(1)}, u32[]{:S(2)}) copy-start(bf16[2,256,8,32]{1,0,3,2:T(2,128)(2,1)S(1)} %reshape.260) | copy-start | bytes 786436
  73.1 68.5 %copy-start.39 = (pred[2,256]{1,0:T(4,128)(4,1)}, pred[2,256]{1,0:T(4,128)(4,1)S(1)}, u32[]{:S(2)}) copy-start(pred[2,256]{1,0:T(4,128)(4,1)S(1)} %broadcast_compare_fusion) | copy-start | bytes 1540
  141.6 16.8 %copy-start.31 = (f32[2,8,256]{2,0,1:T(2,128)}, f32[2,8,256]{2,0,1:T(2,128)S(1)}, u32[]{:S(2)}) copy-start(f32[2,8,256]{2,0,1:T(2,128)S(1)} %psum.50) | copy-start | bytes 49156
  156.2 123.1 %all-gather.7.cloned.1.call-start = ((), (), s32[]{:S(2)}) async-start(), calls=%async_computation.8 | async-start | bytes 4096000 | tf_op jit(solution)/shard_map/all_gather | solution.py:36
  157.0 188.1 %all-gather.9.cloned.1.call-start = ((), (), s32[]{:S(2)}) async-start(), calls=%async_computation.9 | async-start | bytes 4096000 | tf_op jit(solution)/shard_map/all_gather | solution.py:36
  157.6 253.4 %all-gather.11.cloned.1.call-start = ((), (), s32[]{:S(2)}) async-start(), calls=%async_computation.10 | async-start | bytes 4096000 | tf_op jit(solution)/shard_map/all_gather | solution.py:36
  158.1 308.5 %reduce-scatter.9.cloned.1.call-start = ((), (), s32[]{:S(2)}) async-start(), calls=%async_computation.13 | async-start | bytes 491520 | tf_op jit(solution)/shard_map/reduce_scatter | solution.py:40
  158.4 186.7 %copy-start.59 = (f32[1280]{0:T(1024)}, f32[1280]{0:T(1024)S(1)}, u32[]{:S(2)}) copy-start(f32[1280]{0:T(1024)S(1)} %convert_element_type.186) | copy-start | bytes 15364
  158.4 266.3 %copy-start.45 = (f32[1280]{0:T(1024)}, f32[1280]{0:T(1024)S(1)}, u32[]{:S(2)}) copy-start(f32[1280]{0:T(1024)S(1)} %convert_element_type.185) | copy-start | bytes 15364
  216.0 67.3 %copy-start.7 = (bf16[160,8,2,256]{3,1,2,0:T(8,128)(2,1)}, bf16[160,8,2,256]{3,1,2,0:T(8,128)(2,1)S(1)}, u32[]{:S(2)}) copy-start(bf16[160,8,2,256]{3,1,2,0:T(8,128)(2,1)S(1)} %copy.95) | copy-start | bytes 3932164
  283.3 141.4 %copy-start.49 = (f32[512]{0:T(512)}, f32[512]{0:T(512)S(1)}, u32[]{:S(2)}) copy-start(f32[512]{0:T(512)S(1)} %broadcast_multiply_fusion) | copy-start | bytes 6148
  285.1 139.6 %copy-start.61 = (f32[512]{0:T(512)}, f32[512]{0:T(512)S(1)}, u32[]{:S(2)}) copy-start(f32[512]{0:T(512)S(1)} %fusion.45) | copy-start | bytes 6148
  285.2 125.8 %copy-start.24 = (bf16[2,256,1280]{2,1,0:T(8,128)(2,1)S(1)}, bf16[2,256,1280]{2,1,0:T(8,128)(2,1)}, u32[]{:S(2)}) copy-start(bf16[2,256,1280]{2,1,0:T(8,128)(2,1)} %param.31) | copy-start | bytes 3932164
  410.9 11.0 %copy-start.2 = (f32[512,1280]{1,0:T(8,128)S(1)}, f32[512,1280]{1,0:T(8,128)}, u32[]{:S(2)}) copy-start(f32[512,1280]{1,0:T(8,128)} %copy-done.1) | copy-start | bytes 7864324
  410.9 11.0 %copy-start.68 = (bf16[1280,1280]{1,0:T(8,128)(2,1)S(1)}, bf16[1280,1280]{1,0:T(8,128)(2,1)}, u32[]{:S(2)}) copy-start(bf16[1280,1280]{1,0:T(8,128)(2,1)} %all-gather.9.cloned.1.call-done) | copy-start | bytes 9830404
  421.9 2.8 copy-start.71
  425.5 2.9 copy-start.13
  431.3 6.6 copy-start.5
  437.9 2.1 copy-start.23
  440.0 4.2 copy-start.29
  447.2 61.5 %reduce-scatter.11.cloned.1.call-start = ((), (), s32[]{:S(2)}) async-start(), calls=%async_computation.14 | async-start | bytes 2457600 | tf_op jit(solution)/shard_map/reduce_scatter | solution.py:40
  450.1 2.7 copy-start.15
  455.4 181.2 %all-reduce.14.cloned.1.call-start = ((), (), s32[]{:S(2)}) async-start(), calls=%async_computation.12 | async-start | bytes 262144 | tf_op jit(solution)/shard_map/psum | solution.py:135
  457.5 51.3 %copy-start.8 = (bf16[160,8,2,256]{3,1,2,0:T(8,128)(2,1)S(1)}, bf16[160,8,2,256]{3,1,2,0:T(8,128)(2,1)}, u32[]{:S(2)}) copy-start(bf16[160,8,2,256]{3,1,2,0:T(8,128)(2,1)} %copy-done.7) | copy-start | bytes 3932164
  457.5 203.2 %reduce-scatter.7.cloned.1.call-start = ((), (), s32[]{:S(2)}) async-start(), calls=%async_computation.11 | async-start | bytes 819200 | tf_op jit(solution)/shard_map/reduce_scatter | solution.py:40
  460.6 257.1 %all-reduce.16.cloned.1.call-start = ((), (), s32[]{:S(2)}) async-start(), calls=%async_computation.18 | async-start | bytes 1179648 | tf_op jit(solution)/shard_map/psum | solution.py:146
  508.7 273.1 %reduce-scatter.13.cloned.1.call-start = ((), (), s32[]{:S(2)}) async-start(), calls=%async_computation.15 | async-start | bytes 4096000 | tf_op jit(solution)/shard_map/reduce_scatter | solution.py:40
  514.1 332.4 %reduce-scatter.15.cloned.1.call-start = ((), (), s32[]{:S(2)}) async-start(), calls=%async_computation.16 | async-start | bytes 4096000 | tf_op jit(solution)/shard_map/reduce_scatter | solution.py:40
  521.1 390.3 %reduce-scatter.17.cloned.1.call-start = ((), (), s32[]{:S(2)}) async-start(), calls=%async_computation.17 | async-start | bytes 4096000 | tf_op jit(solution)/shard_map/reduce_scatter | solution.py:40
  521.3 4.1 copy-start.25
  530.3 2.9 copy-start.10
  530.3 2.9 copy-start.20
  530.3 2.9 copy-start.35
  530.4 2.9 copy-start.42
  530.4 2.9 copy-start.44
  533.3 41.8 %copy-start.57 = (f32[1280]{0:T(1024)S(1)}, f32[1280]{0:T(1024)}, u32[]{:S(2)}) copy-start(f32[1280]{0:T(1024)} %get-tuple-element.15) | copy-start | bytes 15364
  533.3 41.8 %copy-start.58 = (f32[1280]{0:T(1024)S(1)}, f32[1280]{0:T(1024)}, u32[]{:S(2)}) copy-start(f32[1280]{0:T(1024)} %get-tuple-element.17) | copy-start | bytes 15364
  533.3 60.8 %copy-start.48 = (f32[1,2,2,128]{3,1,2,0:T(2,128)S(1)}, f32[1,2,2,128]{3,1,2,0:T(2,128)}, u32[]{:S(2)}) copy-start(f32[1,2,2,128]{3,1,2,0:T(2,128)} %copy-done.47) | copy-start | bytes 6148
  594.1 2.4 copy-start.27
  596.5 40.1 %copy-start.17 = (bf16[1280,256]{1,0:T(8,128)(2,1)S(1)}, bf16[1280,256]{1,0:T(8,128)(2,1)}, u32[]{:S(2)}) copy-start(bf16[1280,256]{1,0:T(8,128)(2,1)} %copy-done.16) | copy-start | bytes 1966084
  596.5 40.1 %copy-start.38 = (f32[1280]{0:T(1024)S(1)}, f32[1280]{0:T(1024)}, u32[]{:S(2)}) copy-start(f32[1280]{0:T(1024)} %copy-done.37) | copy-start | bytes 15364
  596.5 40.1 %copy-start.52 = (f32[256]{0:T(256)S(1)}, f32[256]{0:T(256)}, u32[]{:S(2)}) copy-start(f32[256]{0:T(256)} %copy-done.51) | copy-start | bytes 3076
  596.5 40.1 %copy-start.54 = (f32[256]{0:T(256)S(1)}, f32[256]{0:T(256)}, u32[]{:S(2)}) copy-start(f32[256]{0:T(256)} %copy-done.53) | copy-start | bytes 3076
  601.5 38.2 %copy-start.56 = (f32[256]{0:T(256)S(1)}, f32[256]{0:T(256)}, u32[]{:S(2)}) copy-start(f32[256]{0:T(256)} %copy-done.55) | copy-start | bytes 3076
  636.6 3.7 copy-start.33
  (22 other events, 27.4 us)
Sparse Core Ops, SparseCore 0:
  9.7 52.2 all-gather.4
  156.4 56.3 all-reduce.11
  214.4 64.8 all-gather.6
  280.8 64.2 all-gather.8
  346.6 64.2 all-gather.10
  447.3 19.2 reduce-scatter.8
  468.9 39.7 reduce-scatter.10
  514.8 121.7 all-reduce.13
  639.5 21.1 reduce-scatter.6
  663.7 53.9 all-reduce.15
  720.2 61.5 reduce-scatter.12
  784.0 62.4 reduce-scatter.14
  848.9 62.3 reduce-scatter.16
where the time goes:
time: 929 us; the launch traced here: 920 us
  waiting for transfers between devices  580 us (62%)
  blocking collectives  175 us (19%)
  matrix products  76.7 us (8%)
  other arithmetic  36.8 us (4%)
  local copies, waits for them, and re-layouts  34.6 us (4%)
  between operations  16.3 us (2%)
    reduce_scatter x6, waiting for transfers between devices, scatter(): lax.psum_scatter(total.astype(LOW), 'wshard', scatter_dimension=0, tiled=...  252 us
    all_gather x4, waiting for transfers between devices, gather(): return lax.all_gather(shard, 'wshard', axis=0, tiled=True)  183 us
    psum x1, waiting for transfers between devices, shards(): lax.psum(scatter(matmul_tn(input_low, dkeys)).astype(LOW), 'ctx')  55.3 us
    psum x1, waiting for transfers between devices, shards(): numer = lax.psum(numer.astype(LOW), 'ctx').astype(FULL)  53.1 us
    all_gather x3, blocking collectives, gather(): return lax.all_gather(shard, 'wshard', axis=0, tiled=True)  53 us
    psum x1, blocking collectives, shards(): in_sums = lax.psum(jnp.concatenate([grad_gin, grad_bin]), ('ctx', 'wshard'))  39.6 us
    psum x1, waiting for transfers between devices, shards(): dquery = lax.psum(dquery.reshape(rows, -1).astype(LOW), ('ctx', 'wshard'))  35.1 us
    psum x1, blocking collectives, shards(): total = lax.psum(jnp.sum(weights, axis=-1), 'ctx')  22.3 us
  transfers between devices with their start and end apart: 13, of which 12 were waited for; matrix products, arithmetic and copies ran while one was open for 10% of the time, Pallas kernels for 0%

commit v1 on v0

--- a/solution.py
+++ b/solution.py
@@ -9,6 +9,18 @@
 FULL = jnp.float32
 
 
+def gather_by_bits(shard, axis, dim):
+    ways, here = (lax.axis_size(axis), lax.axis_index(axis))
+    grown, reach = (shard, 1)
+    while reach < ways:
+        theirs = lax.ppermute(grown, axis, [(d, d ^ reach) for d in range(ways)])
+        mine_first = jnp.concatenate([grown, theirs], axis=dim)
+        theirs_first = jnp.concatenate([theirs, grown], axis=dim)
+        grown = jnp.where(here & reach == 0, mine_first, theirs_first)
+        reach = 2 * reach
+    return grown
+
+
 def layer_norm(values, gain, offset):
     center = jnp.mean(values, axis=-1, keepdims=True)
     centred = values - center
@@ -33,7 +45,7 @@
 
 
 def gather(shard):
-    return lax.all_gather(shard, "wshard", axis=0, tiled=True)
+    return gather_by_bits(shard, "wshard", 0)
 
 
 def scatter(total):

time: 929 us -> 931 us (level)
  blocking collectives: 175 us -> 102 us
  starting transfers between devices: 0.87 us -> 44.7 us
  other arithmetic: 36.8 us -> 56.4 us
  matrix products: 76.7 us -> 89.1 us
  waiting for transfers between devices: 580 us -> 591 us
    ppermute x0 -> x26, waiting for transfers between devices: none -> 199 us  [gather_by_bits(): theirs = lax.ppermute(grown, axis, [(d, d ^ reach) for d in range(ways)])]
    all_gather x4 -> x0, waiting for transfers between devices: 183 us -> none  [gather(): return lax.all_gather(shard, 'wshard', axis=0, tiled=True)]
    all_gather x3 -> x0, blocking collectives: 53 us -> none  [gather(): return lax.all_gather(shard, 'wshard', axis=0, tiled=True)]
    ppermute x0 -> x26, starting transfers between devices: none -> 43.9 us  [gather_by_bits(): theirs = lax.ppermute(grown, axis, [(d, d ^ reach) for d in range(ways)])]
    unnamed x1 -> x0, blocking collectives: 19.8 us -> none
    select_n x0 -> x13, other arithmetic: none -> 18.1 us  [gather_by_bits(): grown = jnp.where(here & reach == 0, mine_first, theirs_first)]
  transfers between devices with their start and end apart: 13 -> 35, of which waited for: 12 -> 24; matrix products, arithmetic and copies ran while one was open for 10% -> 14% of each run, Pallas kernels for 0% -> 0%
where the time goes in v1:
time: 931 us; the launch traced here: 923 us
  waiting for transfers between devices  591 us (63%)
  blocking collectives  102 us (11%)
  matrix products  89.1 us (10%)
  other arithmetic  56.4 us (6%)
  starting transfers between devices  44.7 us (5%)
  local copies, waits for them, and re-layouts  25.4 us (3%)
  between operations  15 us (2%)
    reduce_scatter x6, waiting for transfers between devices, scatter(): lax.psum_scatter(total.astype(LOW), 'wshard', scatter_dimension=0, tiled=...  252 us
    ppermute x26, waiting for transfers between devices, gather_by_bits(): theirs = lax.ppermute(grown, axis, [(d, d ^ reach) for d in range(ways)])  199 us
    psum x1, waiting for transfers between devices, shards(): lax.psum(scatter(matmul_tn(input_low, dkeys)).astype(LOW), 'ctx')  55.3 us
    psum x1, waiting for transfers between devices, shards(): numer = lax.psum(numer.astype(LOW), 'ctx').astype(FULL)  46.5 us
    ppermute x26, starting transfers between devices, gather_by_bits(): theirs = lax.ppermute(grown, axis, [(d, d ^ reach) for d in range(ways)])  43.9 us
    psum x1, blocking collectives, shards(): in_sums = lax.psum(jnp.concatenate([grad_gin, grad_bin]), ('ctx', 'wshard'))  37.8 us
    psum x1, waiting for transfers between devices, shards(): dquery = lax.psum(dquery.reshape(rows, -1).astype(LOW), ('ctx', 'wshard'))  37.5 us
    dot_general x6, matrix products, matmul(): return jnp.dot(left, right, preferred_element_type=FULL)  27 us
  transfers between devices with their start and end apart: 35, of which 24 were waited for; matrix products, arithmetic and copies ran while one was open for 14% of the time, Pallas kernels for 0%

profile of v1, /device:TPU:0, one launch (start us, length us, event | category | flops | bytes accessed | tf_op | source)
XLA Modules:
  0.0 923.1 jit_solution(3374845455109183755)
XLA Ops:
  7.3 3.1 collective-permute-start
  28.4 8.3 collective-permute-done.18
  38.0 2.4 collective-permute-done.20
  40.5 2.6 collective-permute-start.3
  44.9 2.6 collective-permute-start.5
  49.4 2.6 collective-permute-start.11
  52.0 2.4 add_convert_fusion.2
  56.5 2.8 collective-permute-done.13
  61.0 2.9 collective-permute-done.19
  65.6 3.0 collective-permute-done.21
  75.0 34.4 %collective-permute-done.9 = bf16[384,256]{1,0:T(8,128)(2,1)S(1)} collective-permute-done((bf16[384,256]{1,0:T(8,128)(2,1)S(1)}, bf16[384,256]{1,0:T(8,128)(2,1)S(1)}, u32[]{:S(2)}, u32[]{:S(2)}) %collective-permute-start.9) | collective-permute-done | bytes 196640 | tf_op jit(solution)/shard_map/ppermute | solution.py:16
  109.5 3.6 collective-permute-start.24
  113.7 2.8 collective-permute-done.1
  116.5 3.4 collective-permute-start.15
  120.8 9.4 %collective-permute-done.15 = bf16[640,256]{1,0:T(8,128)(2,1)S(1)} collective-permute-done((bf16[640,256]{1,0:T(8,128)(2,1)S(1)}, bf16[640,256]{1,0:T(8,128)(2,1)S(1)}, u32[]{:S(2)}, u32[]{:S(2)}) %collective-permute-start.15) | collective-permute-done | bytes 327712 | tf_op jit(solution)/shard_map/ppermute | solution.py:16
  130.7 3.0 bitcast_reduce_fusion
  133.7 22.3 %pmax.7 = f32[2,8,256]{2,0,1:T(2,128)S(1)} all-reduce(f32[2,8,256]{2,0,1:T(2,128)S(1)} %get-tuple-element.44), channel_id=1, replica_groups=mesh['ctx'=8,'wshard'=4] {'ctx'}, use_global_device_ids=true, to_apply=%region_5.6 | all-reduce | flops 4096 | bytes 32768 | tf_op jit(solution)/shard_map/pmax | solution.py:105
  157.8 3.4 collective-permute-start.7
  161.2 3.4 fusion.39
  164.7 24.1 %psum.50 = f32[2,8,256]{2,0,1:T(2,128)S(1)} all-reduce(f32[2,8,256]{2,0,1:T(2,128)S(1)} %fusion.39), channel_id=1, replica_groups=mesh['ctx'=8,'wshard'=4] {'ctx'}, use_global_device_ids=true, to_apply=%region_8.9 | all-reduce | flops 4096 | bytes 32768 | tf_op jit(solution)/shard_map/psum | solution.py:107
  188.8 4.4 fusion.14
  193.2 3.1 maximum_select_fusion.4
  196.3 42.2 %collective-permute-done.7 = bf16[384,1280]{1,0:T(8,128)(2,1)} collective-permute-done((bf16[384,1280]{1,0:T(8,128)(2,1)S(1)}, bf16[384,1280]{1,0:T(8,128)(2,1)}, u32[]{:S(2)}, u32[]{:S(2)}) %collective-permute-start.7) | collective-permute-done | bytes 983072 | tf_op jit(solution)/shard_map/ppermute | solution.py:16
  238.5 3.8 convolution_convert_fusion.4
  245.2 3.6 fusion.24
  249.0 3.6 maximum_select_fusion.5
  252.5 3.5 maximum_select_fusion.6
  256.0 2.9 collective-permute-start.25
  258.9 46.5 %all-reduce.5.cloned.1.call-done = bf16[2,256,8,160]{1,3,2,0:T(8,128)(2,1)} async-done(((bf16[2,256,8,160]{1,3,2,0:T(8,128)(2,1)}), bf16[2,256,8,160]{1,3,2,0:T(8,128)(2,1)}) %all-reduce.5.cloned.1.call-update) | async-done | bytes 1310736 | tf_op jit(solution)/shard_map/psum | solution.py:109
  308.7 35.2 %collective-permute-done.17 = bf16[640,1280]{1,0:T(8,128)(2,1)} collective-permute-done((bf16[640,1280]{1,0:T(8,128)(2,1)}, bf16[640,1280]{1,0:T(8,128)(2,1)}, u32[]{:S(2)}, u32[]{:S(2)}) %collective-permute-start.17) | collective-permute-done | bytes 1638432 | tf_op jit(solution)/shard_map/ppermute | solution.py:16
  344.0 5.0 fusion.80
  349.4 29.5 %collective-permute-done.23 = bf16[640,1280]{1,0:T(8,128)(2,1)} collective-permute-done((bf16[640,1280]{1,0:T(8,128)(2,1)}, bf16[640,1280]{1,0:T(8,128)(2,1)}, u32[]{:S(2)}, u32[]{:S(2)}) %collective-permute-start.23) | collective-permute-done | bytes 1638432 | tf_op jit(solution)/shard_map/ppermute | solution.py:16
  378.9 11.3 %multiply_convert_fusion.1 = (bf16[512,1280]{1,0:T(8,128)(2,1)}, f32[512,1280]{1,0:T(8,128)S(1)}, f32[512,1280]{1,0:T(8,128)S(1)}) fusion(bf16[640,1280]{1,0:T(8,128)(2,1)} %collective-permute-done.23, bf16[640,1280]{1,0:T(8,128)(2,1)} %maximum_select_fusion.5, pred[]{:T(512)S(6)} %eq.4, f32[512,1280]{1,0:T(8,128)S(1)} %get-tuple-element.47, ...), kind=kOutput, calls=%fused_computation.27 | convolution fusion | flops 1738342400 | bytes 12466177 | tf_op jit(solution)/shard_map/dot_general | solution.py:36
  390.2 22.1 %collective-permute-done.25 = bf16[640,1280]{1,0:T(8,128)(2,1)} collective-permute-done((bf16[640,1280]{1,0:T(8,128)(2,1)}, bf16[640,1280]{1,0:T(8,128)(2,1)}, u32[]{:S(2)}, u32[]{:S(2)}) %collective-permute-start.25) | collective-permute-done | bytes 1638432 | tf_op jit(solution)/shard_map/ppermute | solution.py:16
  412.3 5.8 add_convert_fusion
  418.1 6.5 multiply_reduce_fusion
  427.4 6.2 convolution_convert_fusion.5
  433.6 2.5 copy.70
  436.1 4.0 reshape.583
  442.3 3.8 multiply_convert_fusion
  449.5 2.8 fusion.21
  455.0 2.5 convolution_convert_fusion.3
  457.6 2.0 fusion.34
  459.8 3.1 reduce_sum.204
  462.9 6.5 reduce-scatter.9.cloned.1.call-done
  469.5 42.1 %reduce-scatter.11.cloned.1.call-done = bf16[192,1280]{1,0:T(8,128)(2,1)} async-done(((bf16[768,1280]{1,0:T(8,128)(2,1)}), bf16[192,1280]{1,0:T(8,128)(2,1)}) %reduce-scatter.11.cloned.1.call-update) | async-done | bytes 491536 | tf_op jit(solution)/shard_map/reduce_scatter | solution.py:52
  511.6 5.6 convolution_convert_fusion.1
  518.5 5.3 convolution_convert_fusion.2
  525.2 5.0 convolution_convert_fusion
  530.8 17.4 %psum.55 = f32[2560]{0:T(1024)S(1)} all-reduce(f32[2560]{0:T(1024)S(1)} %pad_maximum_fusion), channel_id=1, replica_groups=mesh['ctx'=8,'wshard'=4] {'wshard'}, use_global_device_ids=true, to_apply=%region_33.34 | all-reduce | flops 2560 | bytes 20480 | tf_op jit(solution)/shard_map/psum | solution.py:162
  549.6 3.5 fusion.41
  554.1 37.8 %psum.52 = f32[1536]{0:T(1024)S(1)} all-reduce(f32[1536]{0:T(1024)S(1)} %pad_maximum_fusion.1), channel_id=1, replica_groups=mesh['ctx'=8,'wshard'=4] {'ctx','wshard'}, use_global_device_ids=true, to_apply=%region_25.26 | all-reduce | flops 1536 | bytes 12288 | tf_op jit(solution)/shard_map/psum | solution.py:160
  595.6 6.1 fusion.2
  601.7 37.5 %all-reduce.7.cloned.1.call-done = bf16[256,256]{0,1:T(8,128)(2,1)} async-done(((bf16[256,256]{0,1:T(8,128)(2,1)}), bf16[256,256]{0,1:T(8,128)(2,1)}) %all-reduce.7.cloned.1.call-update) | async-done | bytes 131088 | tf_op jit(solution)/shard_map/psum | solution.py:147
  643.0 2.0 fusion.46
  644.9 18.2 %reduce-scatter.7.cloned.1.call-done = bf16[64,1280]{1,0:T(8,128)(2,1)} async-done(((bf16[256,1280]{1,0:T(8,128)(2,1)}), bf16[64,1280]{1,0:T(8,128)(2,1)}) %reduce-scatter.7.cloned.1.call-update) | async-done | bytes 163856 | tf_op jit(solution)/shard_map/reduce_scatter | solution.py:52
  664.9 55.3 %all-reduce.9.cloned.1.call-done = (bf16[192,256]{1,0:T(8,128)(2,1)}, bf16[192,1280]{1,0:T(8,128)(2,1)}) async-done(((bf16[192,256]{1,0:T(8,128)(2,1)}, bf16[192,1280]{1,0:T(8,128)(2,1)}), (bf16[192,256]{1,0:T(8,128)(2,1)}, bf16[192,1280]{1,0:T(8,128)(2,1)})) %all-reduce.9.cloned.1.call-update) | async-done | bytes 589840 | tf_op jit(solution)/shard_map/psum | solution.py:158
  720.2 2.0 convert_element_type.240
  723.8 60.4 %reduce-scatter.15.cloned.1.call-done = bf16[320,1280]{1,0:T(8,128)(2,1)} async-done(((bf16[1280,1280]{1,0:T(8,128)(2,1)}), bf16[320,1280]{1,0:T(8,128)(2,1)}) %reduce-scatter.15.cloned.1.call-update) | async-done | bytes 819216 | tf_op jit(solution)/shard_map/reduce_scatter | solution.py:52
  784.2 2.4 convert_element_type.244
  786.6 62.5 %reduce-scatter.13.cloned.1.call-done = bf16[320,1280]{1,0:T(8,128)(2,1)} async-done(((bf16[1280,1280]{1,0:T(8,128)(2,1)}), bf16[320,1280]{1,0:T(8,128)(2,1)}) %reduce-scatter.13.cloned.1.call-update) | async-done | bytes 819216 | tf_op jit(solution)/shard_map/reduce_scatter | solution.py:52
  849.1 2.4 convert_element_type.242
  851.5 62.4 %reduce-scatter.17.cloned.1.call-done = bf16[320,1280]{1,0:T(8,128)(2,1)} async-done(((bf16[1280,1280]{1,0:T(8,128)(2,1)}), bf16[320,1280]{1,0:T(8,128)(2,1)}) %reduce-scatter.17.cloned.1.call-update) | async-done | bytes 819216 | tf_op jit(solution)/shard_map/reduce_scatter | solution.py:52
  914.0 2.4 convert_element_type.246
  (270 shorter events, 72.8 us)
Async XLA Ops:
  7.2 47.2 %copy-start = (bf16[2,256,768]{2,1,0:T(8,128)(2,1)S(1)}, bf16[2,256,768]{2,1,0:T(8,128)(2,1)}, u32[]{:S(2)}) copy-start(bf16[2,256,768]{2,1,0:T(8,128)(2,1)} %param.16) | copy-start | bytes 2359300
  7.2 63.5 %copy-start.34 = (bf16[192,256]{1,0:T(8,128)(2,1)S(1)}, bf16[192,256]{1,0:T(8,128)(2,1)}, u32[]{:S(2)}) copy-start(bf16[192,256]{1,0:T(8,128)(2,1)} %param.24) | copy-start | bytes 294916
  7.2 61.3 %copy-start.20 = (bf16[320,1280]{1,0:T(8,128)(2,1)S(1)}, bf16[320,1280]{1,0:T(8,128)(2,1)}, u32[]{:S(2)}) copy-start(bf16[320,1280]{1,0:T(8,128)(2,1)} %param.26) | copy-start | bytes 2457604
  7.2 298.2 %all-reduce.5.cloned.1.call-start = ((), (), s32[]{:S(2)}) async-start(), calls=%async_computation.6 | async-start | bytes 2621440 | tf_op jit(solution)/shard_map/psum | solution.py:109
  7.3 63.5 %collective-permute-start = (bf16[64,1280]{1,0:T(8,128)(2,1)}, bf16[64,1280]{1,0:T(8,128)(2,1)S(1)}, u32[]{:S(2)}, u32[]{:S(2)}) collective-permute-start(bf16[64,1280]{1,0:T(8,128)(2,1)} %param.18), channel_id=1, source_target_pairs={{0,1},{1,0},{2,3},{3,2},{4,5},{5,4},{6,7},{7,6},{8,9},{9,8},{10,11... | collective-permute-start | bytes 491528 | tf_op jit(solution)/shard_map/ppermute | solution.py:16
  10.3 14.3 %collective-permute-start.10 = (bf16[320]{0:T(512)(128)(2,1)}, bf16[320]{0:T(512)(128)(2,1)S(1)}, u32[]{:S(2)}, u32[]{:S(2)}) collective-permute-start(bf16[320]{0:T(512)(128)(2,1)} %param.19), channel_id=1, source_target_pairs={{0,1},{1,0},{2,3},{3,2},{4,5},{5,4},{6,7},{7,6},{8,9},{9,8},{10,11... | collective-permute-start | bytes 1928 | tf_op jit(solution)/shard_map/ppermute | solution.py:16
  10.4 15.7 %collective-permute-start.12 = (bf16[320]{0:T(512)(128)(2,1)}, bf16[320]{0:T(512)(128)(2,1)S(1)}, u32[]{:S(2)}, u32[]{:S(2)}) collective-permute-start(bf16[320]{0:T(512)(128)(2,1)} %param.20), channel_id=1, source_target_pairs={{0,1},{1,0},{2,3},{3,2},{4,5},{5,4},{6,7},{7,6},{8,9},{9,8},{10,11... | collective-permute-start | bytes 1928 | tf_op jit(solution)/shard_map/ppermute | solution.py:16
  12.4 60.1 %collective-permute-start.14 = (bf16[320,256]{1,0:T(8,128)(2,1)}, bf16[320,256]{1,0:T(8,128)(2,1)}, u32[]{:S(2)}, u32[]{:S(2)}) collective-permute-start(bf16[320,256]{1,0:T(8,128)(2,1)} %param.23), channel_id=1, source_target_pairs={{0,1},{1,0},{2,3},{3,2},{4,5},{5,4},{6,7},{7,6},{8,9},{9,8},{10,11... | collective-permute-start | bytes 491528 | tf_op jit(solution)/shard_map/ppermute | solution.py:16
  12.5 6.2 collective-permute-start.2
  14.4 58.0 %copy-start.29 = (bf16[64,1280]{1,0:T(8,128)(2,1)S(1)}, bf16[64,1280]{1,0:T(8,128)(2,1)}, u32[]{:S(2)}) copy-start(bf16[64,1280]{1,0:T(8,128)(2,1)} %param.18) | copy-start | bytes 491524
  15.8 58.2 %copy-start.30 = (bf16[320,256]{1,0:T(8,128)(2,1)S(1)}, bf16[320,256]{1,0:T(8,128)(2,1)}, u32[]{:S(2)}) copy-start(bf16[320,256]{1,0:T(8,128)(2,1)} %param.23) | copy-start | bytes 491524
  18.1 170.7 %copy-start.39 = (pred[2,256]{1,0:T(4,128)(4,1)}, pred[2,256]{1,0:T(4,128)(4,1)S(1)}, u32[]{:S(2)}) copy-start(pred[2,256]{1,0:T(4,128)(4,1)S(1)} %broadcast_compare_fusion) | copy-start | bytes 1540
  18.7 53.8 %copy-start.43 = (f32[512]{0:T(512)}, f32[512]{0:T(512)S(1)}, u32[]{:S(2)}) copy-start(f32[512]{0:T(512)S(1)} %rsqrt.33) | copy-start | bytes 6148
  18.7 53.8 %copy-start.45 = (f32[1,2,2,128]{3,1,2,0:T(2,128)}, f32[1,2,2,128]{3,1,2,0:T(2,128)S(1)}, u32[]{:S(2)}) copy-start(f32[1,2,2,128]{3,1,2,0:T(2,128)S(1)} %copy.97) | copy-start | bytes 6148
  18.7 3.7 collective-permute-start.4
  22.4 46.6 %collective-permute-start.8 = (bf16[192,256]{1,0:T(8,128)(2,1)}, bf16[192,256]{1,0:T(8,128)(2,1)S(1)}, u32[]{:S(2)}, u32[]{:S(2)}) collective-permute-start(bf16[192,256]{1,0:T(8,128)(2,1)} %param.24), channel_id=1, source_target_pairs={{0,1},{1,0},{2,3},{3,2},{4,5},{5,4},{6,7},{7,6},{8,9},{9,8},{10,11... | collective-permute-start | bytes 294920 | tf_op jit(solution)/shard_map/ppermute | solution.py:16
  24.7 131.4 %collective-permute-start.6 = (bf16[192,1280]{1,0:T(8,128)(2,1)}, bf16[192,1280]{1,0:T(8,128)(2,1)}, u32[]{:S(2)}, u32[]{:S(2)}) collective-permute-start(bf16[192,1280]{1,0:T(8,128)(2,1)} %param.25), channel_id=1, source_target_pairs={{0,1},{1,0},{2,3},{3,2},{4,5},{5,4},{6,7},{7,6},{8,9},{9,8},{10,11... | collective-permute-start | bytes 1474568 | tf_op jit(solution)/shard_map/ppermute | solution.py:16
  26.1 10.6 %collective-permute-start.18 = (bf16[320]{0:T(512)(128)(2,1)}, bf16[320]{0:T(512)(128)(2,1)S(1)}, u32[]{:S(2)}, u32[]{:S(2)}) collective-permute-start(bf16[320]{0:T(512)(128)(2,1)} %param.27), channel_id=1, source_target_pairs={{0,1},{1,0},{2,3},{3,2},{4,5},{5,4},{6,7},{7,6},{8,9},{9,8},{10,11... | collective-permute-start | bytes 1928 | tf_op jit(solution)/shard_map/ppermute | solution.py:16
  36.7 3.8 collective-permute-start.20
  40.5 4.5 collective-permute-start.3
  44.9 4.5 collective-permute-start.5
  49.4 5.4 collective-permute-start.11
  54.7 58.3 %copy-start.21 = (bf16[512,768]{1,0:T(8,128)(2,1)}, bf16[512,768]{1,0:T(8,128)(2,1)S(1)}, u32[]{:S(2)}) copy-start(bf16[512,768]{1,0:T(8,128)(2,1)S(1)} %add_convert_fusion.4) | copy-start | bytes 2359300
  54.8 4.5 collective-permute-start.13
  56.5 63.9 %copy-start.35 = (f32[1280]{0:T(1024)}, f32[1280]{0:T(1024)S(1)}, u32[]{:S(2)}) copy-start(f32[1280]{0:T(1024)S(1)} %fusion.49) | copy-start | bytes 15364
  59.3 4.6 collective-permute-start.19
  63.9 4.6 collective-permute-start.21
  65.5 359.1 %copy-start.41 = (f32[1280]{0:T(1024)}, f32[1280]{0:T(1024)S(1)}, u32[]{:S(2)}) copy-start(f32[1280]{0:T(1024)S(1)} %fusion.51) | copy-start | bytes 15364
  68.5 124.7 %collective-permute-start.16 = (bf16[320,1280]{1,0:T(8,128)(2,1)S(1)}, bf16[320,1280]{1,0:T(8,128)(2,1)}, u32[]{:S(2)}, u32[]{:S(2)}) collective-permute-start(bf16[320,1280]{1,0:T(8,128)(2,1)S(1)} %copy-done.20), channel_id=1, source_target_pairs={{0,1},{1,0},{2,3},{3,2},{4,5},{5,4},{6,7},{7,6},{8,9},{9,8},{10,11... | collective-permute-start | bytes 2457608 | tf_op jit(solution)/shard_map/ppermute | solution.py:16
  69.0 310.0 %copy-start.59 = (f32[1280]{0:T(1024)}, f32[1280]{0:T(1024)S(1)}, u32[]{:S(2)}) copy-start(f32[1280]{0:T(1024)S(1)} %fusion.52) | copy-start | bytes 15364
  69.0 179.9 %collective-permute-start.22 = (bf16[320,1280]{1,0:T(8,128)(2,1)}, bf16[320,1280]{1,0:T(8,128)(2,1)}, u32[]{:S(2)}, u32[]{:S(2)}) collective-permute-start(bf16[320,1280]{1,0:T(8,128)(2,1)} %param.29), channel_id=1, source_target_pairs={{0,1},{1,0},{2,3},{3,2},{4,5},{5,4},{6,7},{7,6},{8,9},{9,8},{10,11... | collective-permute-start | bytes 2457608 | tf_op jit(solution)/shard_map/ppermute | solution.py:16
  70.8 38.7 %collective-permute-start.9 = (bf16[384,256]{1,0:T(8,128)(2,1)S(1)}, bf16[384,256]{1,0:T(8,128)(2,1)S(1)}, u32[]{:S(2)}, u32[]{:S(2)}) collective-permute-start(bf16[384,256]{1,0:T(8,128)(2,1)S(1)} %maximum_select_fusion.21), channel_id=1, source_target_pairs={{0,2},{1,3},{2,0},{3,1},{4,6},{5,7},{6,4},{7,5},{8,10},{9,11},{10,... | collective-permute-start | bytes 589832 | tf_op jit(solution)/shard_map/ppermute | solution.py:16
  72.5 44.0 %collective-permute-start.1 = (bf16[128,1280]{1,0:T(8,128)(2,1)S(1)}, bf16[128,1280]{1,0:T(8,128)(2,1)S(1)}, u32[]{:S(2)}, u32[]{:S(2)}) collective-permute-start(bf16[128,1280]{1,0:T(8,128)(2,1)S(1)} %maximum_select_fusion.19), channel_id=1, source_target_pairs={{0,2},{1,3},{2,0},{3,1},{4,6},{5,7},{6,4},{7,5},{8,10},{9,11},{10,... | collective-permute-start | bytes 983048 | tf_op jit(solution)/shard_map/ppermute | solution.py:16
  75.0 55.2 %copy-start.25 = (bf16[640,256]{1,0:T(8,128)(2,1)}, bf16[640,256]{1,0:T(8,128)(2,1)S(1)}, u32[]{:S(2)}) copy-start(bf16[640,256]{1,0:T(8,128)(2,1)S(1)} %maximum_select_fusion.20) | copy-start | bytes 983044
  109.5 143.1 %collective-permute-start.24 = (bf16[320,1280]{1,0:T(8,128)(2,1)}, bf16[320,1280]{1,0:T(8,128)(2,1)}, u32[]{:S(2)}, u32[]{:S(2)}) collective-permute-start(bf16[320,1280]{1,0:T(8,128)(2,1)} %param.30), channel_id=1, source_target_pairs={{0,1},{1,0},{2,3},{3,2},{4,5},{5,4},{6,7},{7,6},{8,9},{9,8},{10,11... | collective-permute-start | bytes 2457608 | tf_op jit(solution)/shard_map/ppermute | solution.py:16
  116.5 13.7 %collective-permute-start.15 = (bf16[640,256]{1,0:T(8,128)(2,1)S(1)}, bf16[640,256]{1,0:T(8,128)(2,1)S(1)}, u32[]{:S(2)}, u32[]{:S(2)}) collective-permute-start(bf16[640,256]{1,0:T(8,128)(2,1)S(1)} %maximum_select_fusion.20), channel_id=1, source_target_pairs={{0,2},{1,3},{2,0},{3,1},{4,6},{5,7},{6,4},{7,5},{8,10},{9,11},{10,... | collective-permute-start | bytes 983048 | tf_op jit(solution)/shard_map/ppermute | solution.py:16
  157.8 80.7 %copy-start.19 = (bf16[384,1280]{1,0:T(8,128)(2,1)}, bf16[384,1280]{1,0:T(8,128)(2,1)S(1)}, u32[]{:S(2)}) copy-start(bf16[384,1280]{1,0:T(8,128)(2,1)S(1)} %maximum_select_fusion.7) | copy-start | bytes 2949124
  157.8 80.7 %collective-permute-start.7 = (bf16[384,1280]{1,0:T(8,128)(2,1)S(1)}, bf16[384,1280]{1,0:T(8,128)(2,1)}, u32[]{:S(2)}, u32[]{:S(2)}) collective-permute-start(bf16[384,1280]{1,0:T(8,128)(2,1)S(1)} %maximum_select_fusion.7), channel_id=1, source_target_pairs={{0,2},{1,3},{2,0},{3,1},{4,6},{5,7},{6,4},{7,5},{8,10},{9,11},{10,... | collective-permute-start | bytes 2949128 | tf_op jit(solution)/shard_map/ppermute | solution.py:16
  188.8 60.2 %copy-start.31 = (f32[2,8,256]{2,0,1:T(2,128)}, f32[2,8,256]{2,0,1:T(2,128)S(1)}, u32[]{:S(2)}) copy-start(f32[2,8,256]{2,0,1:T(2,128)S(1)} %psum.50) | copy-start | bytes 49156
  193.2 45.3 %copy-start.22 = (bf16[512,768]{1,0:T(8,128)(2,1)S(1)}, bf16[512,768]{1,0:T(8,128)(2,1)}, u32[]{:S(2)}) copy-start(bf16[512,768]{1,0:T(8,128)(2,1)} %copy-done.21) | copy-start | bytes 2359300
  196.3 147.5 %collective-permute-start.17 = (bf16[640,1280]{1,0:T(8,128)(2,1)}, bf16[640,1280]{1,0:T(8,128)(2,1)}, u32[]{:S(2)}, u32[]{:S(2)}) collective-permute-start(bf16[640,1280]{1,0:T(8,128)(2,1)} %maximum_select_fusion.4), channel_id=1, source_target_pairs={{0,2},{1,3},{2,0},{3,1},{4,6},{5,7},{6,4},{7,5},{8,10},{9,11},{10,... | collective-permute-start | bytes 4915208 | tf_op jit(solution)/shard_map/ppermute | solution.py:16
  248.8 220.7 %reduce-scatter.9.cloned.1.call-start = ((), (), s32[]{:S(2)}) async-start(), calls=%async_computation.9 | async-start | bytes 491520 | tf_op jit(solution)/shard_map/reduce_scatter | solution.py:52
  252.5 126.4 %collective-permute-start.23 = (bf16[640,1280]{1,0:T(8,128)(2,1)}, bf16[640,1280]{1,0:T(8,128)(2,1)}, u32[]{:S(2)}, u32[]{:S(2)}) collective-permute-start(bf16[640,1280]{1,0:T(8,128)(2,1)} %maximum_select_fusion.5), channel_id=1, source_target_pairs={{0,2},{1,3},{2,0},{3,1},{4,6},{5,7},{6,4},{7,5},{8,10},{9,11},{10,... | collective-permute-start | bytes 4915208 | tf_op jit(solution)/shard_map/ppermute | solution.py:16
  256.0 156.3 %collective-permute-start.25 = (bf16[640,1280]{1,0:T(8,128)(2,1)}, bf16[640,1280]{1,0:T(8,128)(2,1)}, u32[]{:S(2)}, u32[]{:S(2)}) collective-permute-start(bf16[640,1280]{1,0:T(8,128)(2,1)} %maximum_select_fusion.6), channel_id=1, source_target_pairs={{0,2},{1,3},{2,0},{3,1},{4,6},{5,7},{6,4},{7,5},{8,10},{9,11},{10,... | collective-permute-start | bytes 4915208 | tf_op jit(solution)/shard_map/ppermute | solution.py:16
  349.0 75.7 %copy-start.2 = (f32[512,1280]{1,0:T(8,128)}, f32[512,1280]{1,0:T(8,128)S(1)}, u32[]{:S(2)}) copy-start(f32[512,1280]{1,0:T(8,128)S(1)} %get-tuple-element.47) | copy-start | bytes 7864324
  349.0 75.6 %copy-start.49 = (f32[512]{0:T(512)}, f32[512]{0:T(512)S(1)}, u32[]{:S(2)}) copy-start(f32[512]{0:T(512)S(1)} %broadcast_multiply_fusion) | copy-start | bytes 6148
  349.4 75.2 %copy-start.61 = (f32[512]{0:T(512)}, f32[512]{0:T(512)S(1)}, u32[]{:S(2)}) copy-start(f32[512]{0:T(512)S(1)} %fusion.55) | copy-start | bytes 6148
  349.4 62.8 %copy-start.14 = (bf16[2,256,1280]{2,1,0:T(8,128)(2,1)S(1)}, bf16[2,256,1280]{2,1,0:T(8,128)(2,1)}, u32[]{:S(2)}) copy-start(bf16[2,256,1280]{2,1,0:T(8,128)(2,1)} %param.31) | copy-start | bytes 3932164
  449.0 62.5 %reduce-scatter.11.cloned.1.call-start = ((), (), s32[]{:S(2)}) async-start(), calls=%async_computation.10 | async-start | bytes 2457600 | tf_op jit(solution)/shard_map/reduce_scatter | solution.py:52
  457.6 181.6 %all-reduce.7.cloned.1.call-start = ((), (), s32[]{:S(2)}) async-start(), calls=%async_computation.8 | async-start | bytes 262144 | tf_op jit(solution)/shard_map/psum | solution.py:147
  459.7 51.9 %copy-start.42 = (f32[1280]{0:T(1024)S(1)}, f32[1280]{0:T(1024)}, u32[]{:S(2)}) copy-start(f32[1280]{0:T(1024)} %copy-done.41) | copy-start | bytes 15364
  459.7 51.9 %copy-start.50 = (f32[512]{0:T(512)S(1)}, f32[512]{0:T(512)}, u32[]{:S(2)}) copy-start(f32[512]{0:T(512)} %copy-done.49) | copy-start | bytes 6148
  459.7 51.9 %copy-start.60 = (f32[1280]{0:T(1024)S(1)}, f32[1280]{0:T(1024)}, u32[]{:S(2)}) copy-start(f32[1280]{0:T(1024)} %copy-done.59) | copy-start | bytes 15364
  459.7 52.0 %copy-start.62 = (f32[512]{0:T(512)S(1)}, f32[512]{0:T(512)}, u32[]{:S(2)}) copy-start(f32[512]{0:T(512)} %copy-done.61) | copy-start | bytes 6148
  459.7 52.0 %copy-start.69 = (bf16[512,1280]{1,0:T(8,128)(2,1)S(1)}, bf16[512,1280]{1,0:T(8,128)(2,1)}, u32[]{:S(2)}) copy-start(bf16[512,1280]{1,0:T(8,128)(2,1)} %copy-done.68) | copy-start | bytes 3932164
  459.7 203.4 %reduce-scatter.7.cloned.1.call-start = ((), (), s32[]{:S(2)}) async-start(), calls=%async_computation.7 | async-start | bytes 819200 | tf_op jit(solution)/shard_map/reduce_scatter | solution.py:52
  462.9 257.3 %all-reduce.9.cloned.1.call-start = ((), (), s32[]{:S(2)}) async-start(), calls=%async_computation.14 | async-start | bytes 1179648 | tf_op jit(solution)/shard_map/psum | solution.py:158
  511.6 272.7 %reduce-scatter.15.cloned.1.call-start = ((), (), s32[]{:S(2)}) async-start(), calls=%async_computation.12 | async-start | bytes 4096000 | tf_op jit(solution)/shard_map/reduce_scatter | solution.py:52
  517.2 331.9 %reduce-scatter.13.cloned.1.call-start = ((), (), s32[]{:S(2)}) async-start(), calls=%async_computation.11 | async-start | bytes 4096000 | tf_op jit(solution)/shard_map/reduce_scatter | solution.py:52
  523.9 390.1 %reduce-scatter.17.cloned.1.call-start = ((), (), s32[]{:S(2)}) async-start(), calls=%async_computation.13 | async-start | bytes 4096000 | tf_op jit(solution)/shard_map/reduce_scatter | solution.py:52
  595.6 43.6 %copy-start.36 = (f32[1280]{0:T(1024)S(1)}, f32[1280]{0:T(1024)}, u32[]{:S(2)}) copy-start(f32[1280]{0:T(1024)} %copy-done.35) | copy-start | bytes 15364
  595.6 43.6 %copy-start.52 = (f32[256]{0:T(256)S(1)}, f32[256]{0:T(256)}, u32[]{:S(2)}) copy-start(f32[256]{0:T(256)} %copy-done.51) | copy-start | bytes 3076
  595.6 43.6 %copy-start.54 = (f32[256]{0:T(256)S(1)}, f32[256]{0:T(256)}, u32[]{:S(2)}) copy-start(f32[256]{0:T(256)} %copy-done.53) | copy-start | bytes 3076
  595.6 43.6 %copy-start.64 = (bf16[640,256]{1,0:T(8,128)(2,1)S(1)}, bf16[640,256]{1,0:T(8,128)(2,1)}, u32[]{:S(2)}) copy-start(bf16[640,256]{1,0:T(8,128)(2,1)} %copy-done.63) | copy-start | bytes 983044
  (41 other events, 415.5 us)
Sparse Core Ops, SparseCore 0:
  248.9 56.4 all-reduce.4
  449.1 20.2 reduce-scatter.8
  471.8 39.7 reduce-scatter.10
  517.5 121.6 all-reduce.6
  641.9 21.1 reduce-scatter.6
  666.2 53.9 all-reduce.8
  722.6 61.5 reduce-scatter.14
  786.6 62.4 reduce-scatter.12
  851.5 62.3 reduce-scatter.16
